TPU v7x, 256 devices: a whole 4x4x8 slice. The times are simulated.
256 devices in a mesh: lon: 8 (over y, x_lo), lat: 16 (over z, x_hi), rep: 2 (over core).
Axes of the slice: x: 4 (x_hi: 2, x_lo: 2; x = x_hi * 2 + x_lo), y: 4, z: 8, core: 2. Of those that a mesh axis runs over, the one named last changes fastest.
Arguments:
- forcing: float32 [8, 4, 2, 512, 2048], P('rep', None, None, 'lat', 'lon'), may hold values from -6 to 6
- diffusivity: float32 [512, 2048], P('lat', 'lon'), may hold values from 0.1 to 0.22
- ocean: int32 [512, 2048], P('lat', 'lon'), may hold values 0 or 1
- phase: float32 [4], replicated, may hold values from 0.1 to 0.4
- site_cell: int32 [16, 8, 2048], P('lat', 'lon'), may hold values from 0 to 8191
- site_count: int32 [16, 8], P('lat', 'lon'), may hold values from 1 to 2048, 10240 in all within a row
- site_weight: float32 [16, 8, 2048], P('lat', 'lon'), may hold values from 0.5 to 5
Outputs:
- representer: float32 [8, 4, 2, 512, 2048], P('rep', None, None, 'lat', 'lon')
- gram: float32 [8, 8], P('rep')
Inputs may be any that keep to these rules, and one draw needn't show every extreme that they name: `site_count`: live slots are the first ones of a block; in each latitude row of blocks one block has all 2048 slots live.
All inputs are finite; a program needn't handle non-finite values. No bound on the sum of `ocean` on one device may be relied on, other than what follows from the above.
Results may differ from a plain program's by a relative error of at most 0.00007.
Values sent between devices are 32-bit elements; how exact they have to be, the bound alone decides.
A program may use at most 64 MiB of HBM per device.

v0:
```python
import jax
import jax.numpy as jnp
from jax import lax
from jax.sharding import Mesh
from jax.sharding import PartitionSpec as P

CONST = 4
SWEEPS = 4
LAT = ("lat_0", "lat_1")
LON_LAT = ("lon_0", "lon_1", "lat_0", "lat_1")
LON = ("lon_0", "lon_1")
DAMPING = 0.9


def padded_2(shard, sides, width):
    for axis, dim in sides:
        devices, length = (lax.axis_size(axis), shard.shape[dim])
        up = [(i, (i + 1) % devices) for i in range(devices)]
        down = [(j, i) for i, j in up]
        last = lax.slice_in_dim(shard, length - width, length, axis=dim)
        leading = lax.slice_in_dim(shard, 0, width, axis=dim)
        before = lax.ppermute(last, axis, up)
        after = lax.ppermute(leading, axis, down)
        shard = jnp.concatenate([before, shard, after], axis=dim)
    return shard


def copy_for_each(shard, axis):
    copies = jnp.broadcast_to(shard, (lax.axis_size(axis), *shard.shape))
    return lax.all_to_all(copies, axis, split_axis=0, concat_axis=0, tiled=True)


def laid_out(pieces, dim):
    pieces = jnp.moveaxis(pieces, 0, dim)
    dims = pieces.shape
    return pieces.reshape(*dims[:dim], dims[dim] * dims[dim + 1], *dims[dim + 2 :])


def gather_directly(shard, axis, dim):
    pieces = copy_for_each(shard, axis)
    return laid_out(pieces, dim)


def one_axis_at_a_time(shard, axes):
    for axis in axes:
        shard = lax.psum(shard, axis)
    return shard


def laplace(padded):
    center = padded[..., 1:-1, 1:-1]
    total = (
        padded[..., 2:, 1:-1]
        + padded[..., :-2, 1:-1]
        + padded[..., 1:-1, 2:]
        + padded[..., 1:-1, :-2]
    )
    return total - 4.0 * center


def rotate(field, cosine, sinus):
    real_part = field[:, :, 0]
    imag_part = field[:, :, 1]
    new_real = cosine * real_part - sinus * imag_part
    new_imag = sinus * real_part + cosine * imag_part
    return jnp.stack([new_real, new_imag], axis=2)


def lat_valid(rows_lat, width):
    first = lax.axis_index(LAT) * rows_lat - width
    latitude = first + jnp.arange(rows_lat + 2 * width, dtype=jnp.int32)
    inside = (latitude >= 0) & (latitude < rows_lat * lax.axis_size(LAT))
    return inside.astype(jnp.float32)[:, None]


def local(forcing, diffusivity, ocean, phase, site_cell, site_count, site_weight):
    rows_lat = forcing.shape[3]
    cols_lon = forcing.shape[4]
    wet = ocean.astype(jnp.float32)
    cosine = jnp.cos(phase)[:, None, None]
    sinus = jnp.sin(phase)[:, None, None]
    depth = SWEEPS
    deep_valid = lat_valid(rows_lat, depth)
    coefficients = jnp.stack([diffusivity, wet], axis=0)
    extended = padded_2(coefficients, ((LON, 2), (LAT, 1)), depth) * deep_valid
    diffuse_ext = extended[0]
    wet_ext = extended[1]

    def window(array, width):
        start = depth - width
        return array[start : start + rows_lat + 2 * width, start : start + cols_lon + 2 * width]

    current = padded_2(forcing, ((LON, 4), (LAT, 3)), depth) * deep_valid
    for step in range(SWEEPS):
        width = depth - step
        product = window(diffuse_ext, width) * current
        inner = current[..., 1:-1, 1:-1]
        current = window(wet_ext, width - 1) * (
            DAMPING * rotate(inner, cosine, -sinus) + laplace(product)
        )
    current = padded_2(current, ((LON, 4), (LAT, 3)), depth) * deep_valid
    for step in range(SWEEPS):
        width = depth - step
        inner = current[..., 1:-1, 1:-1]
        current = window(wet_ext, width - 1) * (
            DAMPING * rotate(inner, cosine, sinus)
            + window(diffuse_ext, width - 1) * laplace(current)
        )
    rep_local = current.shape[0]
    slot_total = site_cell.shape[2]
    flat = current.reshape(rep_local, CONST * 2, rows_lat * cols_lon)
    samples = jnp.take(flat, site_cell[0, 0], axis=2)
    slots = jnp.arange(slot_total, dtype=jnp.int32)
    weight = site_weight[0, 0] * (slots < site_count[0, 0]).astype(jnp.float32)
    weighted = (samples * weight[None, None, :]).reshape(rep_local, -1)
    plain = samples.reshape(rep_local, -1)
    gathered = gather_directly(plain, "rep", 0)
    partial_rows = jnp.dot(
        weighted, gathered.T, precision=lax.Precision.HIGHEST, preferred_element_type=jnp.float32
    )
    scale = float(lax.axis_size(LAT) * lax.axis_size(LON) * slot_total)
    gram = one_axis_at_a_time(partial_rows, LON_LAT) / scale
    return (current, gram)


def solution(mesh):
    torus = Mesh(
        mesh.devices.reshape(4, 2, 8, 2, mesh.shape["rep"]),
        ("lon_0", "lon_1", "lat_0", "lat_1", "rep"),
    )
    return jax.shard_map(
        local,
        mesh=torus,
        in_specs=(
            P("rep", None, None, LAT, LON),
            P(LAT, LON),
            P(LAT, LON),
            P(),
            P(LAT, LON, None),
            P(LAT, LON),
            P(LAT, LON, None),
        ),
        out_specs=(P("rep", None, None, LAT, LON), P("rep", None)),
        check_vma=False,
    )
```

profile of v0, /device:TPU:2, one launch (start us, length us, event | category | flops | bytes accessed | tf_op | source)
XLA Modules:
  0.0 189.4 jit_solution(609035854693240836)
XLA Ops:
  0.7 0.8 convert_bitcast_fusion
  1.5 0.8 fusion.30
  2.3 1.6 collective-permute-start
  3.9 0.8 collective-permute-start.1
  4.7 1.4 fusion.35
  6.1 2.2 %collective-permute-start.4 = (f32[4,4,2,32,4]{4,3,2,1,0:T(8,128)S(1)}, f32[4,4,2,32,4]{4,3,2,1,0:T(8,128)S(1)}, u32[]{:S(2)}, u32[]{:S(2)}) collective-permute-start(f32[4,4,2,32,4]{4,3,2,1,0:T(8,128)S(1)} %get-tuple-element.32), channel_id=1, source_target_pairs={{0,32},{32,64},{64,96},{96,128},{128,160},{160,192},{192,224},{224... | collective-permute-start | bytes 49160 | tf_op jit(solution)/shard_map/ppermute | solution.py:22
  8.3 2.0 %collective-permute-start.5 = (f32[4,4,2,32,4]{4,3,2,1,0:T(8,128)S(1)}, f32[4,4,2,32,4]{4,3,2,1,0:T(8,128)S(1)}, u32[]{:S(2)}, u32[]{:S(2)}) collective-permute-start(f32[4,4,2,32,4]{4,3,2,1,0:T(8,128)S(1)} %get-tuple-element.33), channel_id=1, source_target_pairs={{32,0},{64,32},{96,64},{128,96},{160,128},{192,160},{224,192},{0,2... | collective-permute-start | bytes 49160 | tf_op jit(solution)/shard_map/ppermute | solution.py:23
  11.1 0.1 pad_maximum_fusion.10
  11.2 0.8 collective-permute-start.2
  12.0 5.4 %collective-permute-start.3 = (f32[2,4,264]{2,1,0:T(4,128)S(1)}, f32[2,4,264]{2,1,0:T(4,128)S(1)}, u32[]{:S(2)}, u32[]{:S(2)}) collective-permute-start(f32[2,4,264]{2,1,0:T(4,128)S(1)} %get-tuple-element.35), channel_id=1, source_target_pairs={{2,0},{4,2},{6,4},{8,6},{10,8},{12,10},{14,12},{16,14},{18,16},{20... | collective-permute-start | bytes 25352 | tf_op jit(solution)/shard_map/ppermute | solution.py:23
  17.4 13.3 %collective-permute-done.2 = f32[2,4,264]{2,1,0:T(4,128)S(1)} collective-permute-done((f32[2,4,264]{2,1,0:T(4,128)S(1)}, f32[2,4,264]{2,1,0:T(4,128)S(1)}, u32[]{:S(2)}, u32[]{:S(2)}) %collective-permute-start.2) | collective-permute-done | bytes 8480 | tf_op jit(solution)/shard_map/ppermute | solution.py:22
  30.7 2.9 %collective-permute-done.3 = f32[2,4,264]{2,1,0:T(4,128)S(1)} collective-permute-done((f32[2,4,264]{2,1,0:T(4,128)S(1)}, f32[2,4,264]{2,1,0:T(4,128)S(1)}, u32[]{:S(2)}, u32[]{:S(2)}) %collective-permute-start.3) | collective-permute-done | bytes 8480 | tf_op jit(solution)/shard_map/ppermute | solution.py:23
  33.6 0.1 maximum_multiply_fusion.10
  33.7 0.3 pad_maximum_fusion.5
  34.1 1.2 collective-permute-start.6
  35.3 5.6 %collective-permute-start.7 = (f32[4,4,2,4,264]{4,3,2,1,0:T(4,128)S(1)}, f32[4,4,2,4,264]{4,3,2,1,0:T(4,128)S(1)}, u32[]{:S(2)}, u32[]{:S(2)}) collective-permute-start(f32[4,4,2,4,264]{4,3,2,1,0:T(4,128)S(1)} %get-tuple-element.13), channel_id=1, source_target_pairs={{2,0},{4,2},{6,4},{8,6},{10,8},{12,10},{14,12},{16,14},{18,16},{20... | collective-permute-start | bytes 405512 | tf_op jit(solution)/shard_map/ppermute | solution.py:23
  40.8 0.1 slice.362
  41.0 0.1 slice.351
  41.4 2.8 %collective-permute-done.6 = f32[4,4,2,4,264]{4,3,2,1,0:T(4,128)S(1)} collective-permute-done((f32[4,4,2,4,264]{4,3,2,1,0:T(4,128)S(1)}, f32[4,4,2,4,264]{4,3,2,1,0:T(4,128)S(1)}, u32[]{:S(2)}, u32[]{:S(2)}) %collective-permute-start.6) | collective-permute-done | bytes 135200 | tf_op jit(solution)/shard_map/ppermute | solution.py:22
  44.2 2.0 %collective-permute-done.7 = f32[4,4,2,4,264]{4,3,2,1,0:T(4,128)S(1)} collective-permute-done((f32[4,4,2,4,264]{4,3,2,1,0:T(4,128)S(1)}, f32[4,4,2,4,264]{4,3,2,1,0:T(4,128)S(1)}, u32[]{:S(2)}, u32[]{:S(2)}) %collective-permute-start.7) | collective-permute-done | bytes 135200 | tf_op jit(solution)/shard_map/ppermute | solution.py:23
  46.2 1.0 broadcast_multiply_fusion.3
  47.2 0.6 multiply_subtract_fusion.5
  47.8 2.1 %broadcast_multiply_fusion.2 = (f32[4,4,2,38,262]{4,3,2,1,0:T(8,128)S(1)}, f32[4,4,2,38,262]{4,3,2,1,0:T(8,128)S(1)}) fusion(f32[38,262]{1,0:T(8,128)S(1)} %slice.362, f32[4,4,2,40,264]{4,3,2,1,0:T(8,128)S(1)} %get-tuple-element.8, f32[4,4,1,38,262]{4,3,2,1,0:T(8,128)S(1)} %get-tuple-element.29, f32[4,4,1,38,262]{4,3,2,1,0:T(8,128)S(1)} %get-tuple-element.28, ...), kind=kLoop, calls=%fused_computation.81 | loop fusion | flops 3185920 | bytes 10274592 | tf_op jit(solution)/shard_map/mul | solution.py:96
  50.0 0.6 multiply_subtract_fusion.4
  50.6 2.1 %broadcast_multiply_fusion.1 = (f32[4,4,2,36,260]{4,3,2,1,0:T(8,128)S(1)}, f32[4,4,2,36,260]{4,3,2,1,0:T(8,128)S(1)}) fusion(f32[36,260]{1,0:T(8,128)S(1)} %slice.370, f32[4,4,2,38,262]{4,3,2,1,0:T(8,128)S(1)} %get-tuple-element.6, f32[4,4,1,36,260]{4,3,2,1,0:T(8,128)S(1)} %get-tuple-element.27, f32[4,4,1,36,260]{4,3,2,1,0:T(8,128)S(1)} %get-tuple-element.26, ...), kind=kLoop, calls=%fused_computation.78 | loop fusion | flops 2995200 | bytes 9659520 | tf_op jit(solution)/shard_map/mul | solution.py:96
  52.7 0.6 multiply_subtract_fusion.3
  53.4 2.1 %broadcast_multiply_fusion = (f32[4,4,2,34,258]{4,3,2,1,0:T(8,128)S(1)}, f32[4,4,2,34,258]{4,3,2,1,0:T(8,128)S(1)}) fusion(f32[34,258]{1,0:T(8,128)S(1)} %slice.378, f32[4,4,2,36,260]{4,3,2,1,0:T(8,128)S(1)} %get-tuple-element.4, f32[4,4,1,34,258]{4,3,2,1,0:T(8,128)S(1)} %get-tuple-element.25, f32[4,4,1,34,258]{4,3,2,1,0:T(8,128)S(1)} %get-tuple-element.24, ...), kind=kLoop, calls=%fused_computation.77 | loop fusion | flops 2807040 | bytes 9052704 | tf_op jit(solution)/shard_map/mul | solution.py:96
  55.5 0.4 multiply_subtract_fusion.7
  55.9 1.2 fusion.27
  57.1 0.2 fusion.34
  57.3 2.1 %collective-permute-start.8 = (f32[4,4,2,32,4]{4,3,2,1,0:T(8,128)S(1)}, f32[4,4,2,32,4]{4,3,2,1,0:T(8,128)S(1)}, u32[]{:S(2)}, u32[]{:S(2)}) collective-permute-start(f32[4,4,2,32,4]{4,3,2,1,0:T(8,128)S(1)} %get-tuple-element.30), channel_id=1, source_target_pairs={{0,32},{32,64},{64,96},{96,128},{128,160},{160,192},{192,224},{224... | collective-permute-start | bytes 49160 | tf_op jit(solution)/shard_map/ppermute | solution.py:22
  59.5 12.7 %collective-permute-done.8 = f32[4,4,2,32,4]{4,3,2,1,0:T(8,128)S(1)} collective-permute-done((f32[4,4,2,32,4]{4,3,2,1,0:T(8,128)S(1)}, f32[4,4,2,32,4]{4,3,2,1,0:T(8,128)S(1)}, u32[]{:S(2)}, u32[]{:S(2)}) %collective-permute-start.8) | collective-permute-done | bytes 16416 | tf_op jit(solution)/shard_map/ppermute | solution.py:22
  72.2 11.3 %collective-permute-done.9 = f32[4,4,2,32,4]{4,3,2,1,0:T(8,128)S(1)} collective-permute-done((f32[4,4,2,32,4]{4,3,2,1,0:T(8,128)S(1)}, f32[4,4,2,32,4]{4,3,2,1,0:T(8,128)S(1)}, u32[]{:S(2)}, u32[]{:S(2)}) %collective-permute-start.9) | collective-permute-done | bytes 16416 | tf_op jit(solution)/shard_map/ppermute | solution.py:23
  83.5 0.3 pad_maximum_fusion.2
  83.9 0.1 collective-permute-start.10
  84.0 5.6 %collective-permute-start.11 = (f32[4,4,2,4,264]{4,3,2,1,0:T(4,128)S(1)}, f32[4,4,2,4,264]{4,3,2,1,0:T(4,128)S(1)}, u32[]{:S(2)}, u32[]{:S(2)}) collective-permute-start(f32[4,4,2,4,264]{4,3,2,1,0:T(4,128)S(1)} %get-tuple-element.11), channel_id=1, source_target_pairs={{2,0},{4,2},{6,4},{8,6},{10,8},{12,10},{14,12},{16,14},{18,16},{20... | collective-permute-start | bytes 405512 | tf_op jit(solution)/shard_map/ppermute | solution.py:23
  89.7 3.7 %collective-permute-done.10 = f32[4,4,2,4,264]{4,3,2,1,0:T(4,128)S(1)} collective-permute-done((f32[4,4,2,4,264]{4,3,2,1,0:T(4,128)S(1)}, f32[4,4,2,4,264]{4,3,2,1,0:T(4,128)S(1)}, u32[]{:S(2)}, u32[]{:S(2)}) %collective-permute-start.10) | collective-permute-done | bytes 135200 | tf_op jit(solution)/shard_map/ppermute | solution.py:22
  93.3 0.8 collective-permute-done.11
  94.2 0.9 maximum_multiply_fusion.4
  95.0 0.6 multiply_subtract_fusion.2
  95.7 2.2 %fusion.11 = f32[4,4,2,38,262]{4,3,2,1,0:T(8,128)S(1)} fusion(f32[4,4,2,40,264]{4,3,2,1,0:T(8,128)S(1)} %maximum_multiply_fusion.4, f32[4,4,1,38,262]{4,3,2,1,0:T(8,128)S(1)} %get-tuple-element.21, f32[4,4,1,38,262]{4,3,2,1,0:T(8,128)S(1)} %get-tuple-element.20, f32[38,262]{1,0:T(8,128)S(1)} %slice.362, f32[38,262]{1,0:T(8,128)S(1)} %slice.351), kind=kLoop, calls=%fused_computation.21 | loop fusion | flops 3185920 | bytes 9000224 | tf_op jit(solution)/shard_map/mul | solution.py:105
  97.8 0.6 multiply_subtract_fusion.1
  98.5 2.2 %fusion.7 = f32[4,4,2,36,260]{4,3,2,1,0:T(8,128)S(1)} fusion(f32[4,4,2,38,262]{4,3,2,1,0:T(8,128)S(1)} %fusion.11, f32[4,4,1,36,260]{4,3,2,1,0:T(8,128)S(1)} %get-tuple-element.19, f32[4,4,1,36,260]{4,3,2,1,0:T(8,128)S(1)} %get-tuple-element.18, f32[36,260]{1,0:T(8,128)S(1)} %slice.370, f32[36,260]{1,0:T(8,128)S(1)} %slice.350), kind=kLoop, calls=%fused_computation.13 | loop fusion | flops 2995200 | bytes 8461440 | tf_op jit(solution)/shard_map/mul | solution.py:105
  100.7 0.6 multiply_subtract_fusion
  101.3 2.2 %fusion.3 = f32[4,4,2,34,258]{4,3,2,1,0:T(8,128)S(1)} fusion(f32[4,4,2,36,260]{4,3,2,1,0:T(8,128)S(1)} %fusion.7, f32[4,4,1,34,258]{4,3,2,1,0:T(8,128)S(1)} %get-tuple-element.17, f32[4,4,1,34,258]{4,3,2,1,0:T(8,128)S(1)} %get-tuple-element.16, f32[34,258]{1,0:T(8,128)S(1)} %slice.378, f32[34,258]{1,0:T(8,128)S(1)} %slice.349), kind=kLoop, calls=%fused_computation.5 | loop fusion | flops 2807040 | bytes 7929888 | tf_op jit(solution)/shard_map/mul | solution.py:105
  103.5 0.4 multiply_subtract_fusion.6
  103.9 1.2 fusion.24
  105.1 0.2 reshape.141
  105.3 10.9 %copy.13 = f32[4,8,8192]{1,0,2:T(4,128)} copy(f32[4,8,8192]{2,1,0:T(8,128)S(1)} %reshape.141) | data formatting | bytes 2097152 | tf_op jit(solution)/shard_map/reshape | solution.py:111
  116.2 21.1 %gather_fusion = f32[2048,4,8]{2,1,0:T(4,128)} fusion(f32[4,8,8192]{1,0,2:T(4,128)} %copy.13, s32[2048]{0:T(1024)S(1)} %broadcast_clamp_fusion), kind=kCustom, calls=%fused_computation | custom fusion | bytes 532480 | tf_op jit(solution)/shard_map/jit(_take)/gather | solution.py:112
  137.3 3.4 %copy.14 = f32[2048,4,8]{0,2,1:T(8,128)S(1)} copy(f32[2048,4,8]{2,1,0:T(4,128)} %gather_fusion) | data formatting | bytes 524288 | tf_op jit(solution)/shard_map/jit(_take)/gather | solution.py:112
  140.7 0.2 copy.17
  140.9 0.1 broadcast_select_fusion
  141.0 0.9 broadcast_in_dim.23
  141.9 3.5 %all-to-all-start = ((f32[2,4,16384]{2,1,0:T(4,128)}), f32[2,4,16384]{2,1,0:T(4,128)S(1)}, u32[]{:S(2)}, u32[]{:S(2)}) async-start(f32[2,4,16384]{2,1,0:T(4,128)} %broadcast_in_dim.23), calls=%async_computation | async-start | bytes 1048576 | tf_op jit(solution)/shard_map/all_to_all | solution.py:30
  145.4 0.2 copy.15
  145.6 1.5 all-to-all-done
  147.1 0.2 reshape.142
  147.3 1.3 fusion.37
  148.6 10.6 %psum.28 = f32[4,8]{1,0:T(4,128)S(1)} all-reduce(f32[4,8]{1,0:T(4,128)S(1)} %fusion.37), channel_id=1, replica_groups=mesh['lon_0'=4,'lon_1'=2,'lat_0'=8,'lat_1'=2,'rep'=2] {'lon_0'}, use_global_device_ids=true, to_apply=%region_0.1 | all-reduce | flops 32 | bytes 256 | tf_op jit(solution)/shard_map/psum | solution.py:46
  159.2 4.9 %psum.29 = f32[4,8]{1,0:T(4,128)S(1)} all-reduce(f32[4,8]{1,0:T(4,128)S(1)} %psum.28), channel_id=1, replica_groups=mesh['lon_0'=4,'lon_1'=2,'lat_0'=8,'lat_1'=2,'rep'=2] {'lon_1'}, use_global_device_ids=true, to_apply=%region_1.2 | all-reduce | flops 32 | bytes 256 | tf_op jit(solution)/shard_map/psum | solution.py:46
  164.1 18.3 %psum.30 = f32[4,8]{1,0:T(4,128)S(1)} all-reduce(f32[4,8]{1,0:T(4,128)S(1)} %psum.29), channel_id=1, replica_groups=mesh['lon_0'=4,'lon_1'=2,'lat_0'=8,'lat_1'=2,'rep'=2] {'lat_0'}, use_global_device_ids=true, to_apply=%region_2.3 | all-reduce | flops 32 | bytes 256 | tf_op jit(solution)/shard_map/psum | solution.py:46
  182.4 6.4 %psum.31 = f32[4,8]{1,0:T(4,128)S(1)} all-reduce(f32[4,8]{1,0:T(4,128)S(1)} %psum.30), channel_id=1, replica_groups=mesh['lon_0'=4,'lon_1'=2,'lat_0'=8,'lat_1'=2,'rep'=2] {'lat_1'}, use_global_device_ids=true, to_apply=%region_3.4 | all-reduce | flops 32 | bytes 256 | tf_op jit(solution)/shard_map/psum | solution.py:46
  188.8 0.6 broadcast_multiply_fusion.4
  (34 shorter events, 0.7 us)
Async XLA Ops:
  0.6 10.5 %copy-start.2 = (f32[32,256]{1,0:T(8,128)S(1)}, f32[32,256]{1,0:T(8,128)}, u32[]{:S(2)}) copy-start(f32[32,256]{1,0:T(8,128)} %param.8) | copy-start | bytes 98308
  0.6 33.1 %copy-start = (f32[4,4,2,32,256]{4,3,2,1,0:T(8,128)S(1)}, f32[4,4,2,32,256]{4,3,2,1,0:T(8,128)}, u32[]{:S(2)}) copy-start(f32[4,4,2,32,256]{4,3,2,1,0:T(8,128)} %param.7) | copy-start | bytes 3145732
  0.7 9.7 %copy-start.3 = (s32[1,1,2048]{2,1,0:T(1,128)S(1)}, s32[1,1,2048]{2,1,0:T(1,128)}, u32[]{:S(2)}) copy-start(s32[1,1,2048]{2,1,0:T(1,128)} %param.11) | copy-start | bytes 24580
  0.7 10.3 %copy-start.4 = (f32[1,1,2048]{2,1,0:T(1,128)S(1)}, f32[1,1,2048]{2,1,0:T(1,128)}, u32[]{:S(2)}) copy-start(f32[1,1,2048]{2,1,0:T(1,128)} %param.13) | copy-start | bytes 24580
  0.7 10.3 %copy-start.5 = (f32[4]{0:T(128)S(1)}, f32[4]{0:T(128)}, u32[]{:S(2)}) copy-start(f32[4]{0:T(128)} %param.10) | copy-start | bytes 52
  2.3 8.7 %collective-permute-start = (f32[2,32,4]{2,1,0:T(8,128)S(1)}, f32[2,32,4]{2,1,0:T(8,128)S(1)}, u32[]{:S(2)}, u32[]{:S(2)}) collective-permute-start(f32[2,32,4]{2,1,0:T(8,128)S(1)} %get-tuple-element.38), channel_id=1, source_target_pairs={{0,32},{32,64},{64,96},{96,128},{128,160},{160,192},{192,224},{224... | collective-permute-start | bytes 3080 | tf_op jit(solution)/shard_map/ppermute | solution.py:22
  3.9 7.2 %collective-permute-start.1 = (f32[2,32,4]{2,1,0:T(8,128)S(1)}, f32[2,32,4]{2,1,0:T(8,128)S(1)}, u32[]{:S(2)}, u32[]{:S(2)}) collective-permute-start(f32[2,32,4]{2,1,0:T(8,128)S(1)} %get-tuple-element.39), channel_id=1, source_target_pairs={{32,0},{64,32},{96,64},{128,96},{160,128},{192,160},{224,192},{0,2... | collective-permute-start | bytes 3080 | tf_op jit(solution)/shard_map/ppermute | solution.py:23
  6.1 27.6 %collective-permute-start.4 = (f32[4,4,2,32,4]{4,3,2,1,0:T(8,128)S(1)}, f32[4,4,2,32,4]{4,3,2,1,0:T(8,128)S(1)}, u32[]{:S(2)}, u32[]{:S(2)}) collective-permute-start(f32[4,4,2,32,4]{4,3,2,1,0:T(8,128)S(1)} %get-tuple-element.32), channel_id=1, source_target_pairs={{0,32},{32,64},{64,96},{96,128},{128,160},{160,192},{192,224},{224... | collective-permute-start | bytes 49160 | tf_op jit(solution)/shard_map/ppermute | solution.py:22
  8.3 25.4 %collective-permute-start.5 = (f32[4,4,2,32,4]{4,3,2,1,0:T(8,128)S(1)}, f32[4,4,2,32,4]{4,3,2,1,0:T(8,128)S(1)}, u32[]{:S(2)}, u32[]{:S(2)}) collective-permute-start(f32[4,4,2,32,4]{4,3,2,1,0:T(8,128)S(1)} %get-tuple-element.33), channel_id=1, source_target_pairs={{32,0},{64,32},{96,64},{128,96},{160,128},{192,160},{224,192},{0,2... | collective-permute-start | bytes 49160 | tf_op jit(solution)/shard_map/ppermute | solution.py:23
  11.2 19.5 %collective-permute-start.2 = (f32[2,4,264]{2,1,0:T(4,128)S(1)}, f32[2,4,264]{2,1,0:T(4,128)S(1)}, u32[]{:S(2)}, u32[]{:S(2)}) collective-permute-start(f32[2,4,264]{2,1,0:T(4,128)S(1)} %get-tuple-element.34), channel_id=1, source_target_pairs={{0,2},{2,4},{4,6},{6,8},{8,10},{10,12},{12,14},{14,16},{16,18},{18... | collective-permute-start | bytes 25352 | tf_op jit(solution)/shard_map/ppermute | solution.py:22
  12.0 21.6 %collective-permute-start.3 = (f32[2,4,264]{2,1,0:T(4,128)S(1)}, f32[2,4,264]{2,1,0:T(4,128)S(1)}, u32[]{:S(2)}, u32[]{:S(2)}) collective-permute-start(f32[2,4,264]{2,1,0:T(4,128)S(1)} %get-tuple-element.35), channel_id=1, source_target_pairs={{2,0},{4,2},{6,4},{8,6},{10,8},{12,10},{14,12},{16,14},{18,16},{20... | collective-permute-start | bytes 25352 | tf_op jit(solution)/shard_map/ppermute | solution.py:23
  34.1 10.1 %collective-permute-start.6 = (f32[4,4,2,4,264]{4,3,2,1,0:T(4,128)S(1)}, f32[4,4,2,4,264]{4,3,2,1,0:T(4,128)S(1)}, u32[]{:S(2)}, u32[]{:S(2)}) collective-permute-start(f32[4,4,2,4,264]{4,3,2,1,0:T(4,128)S(1)} %get-tuple-element.12), channel_id=1, source_target_pairs={{0,2},{2,4},{4,6},{6,8},{8,10},{10,12},{12,14},{14,16},{16,18},{18... | collective-permute-start | bytes 405512 | tf_op jit(solution)/shard_map/ppermute | solution.py:22
  35.3 10.9 %collective-permute-start.7 = (f32[4,4,2,4,264]{4,3,2,1,0:T(4,128)S(1)}, f32[4,4,2,4,264]{4,3,2,1,0:T(4,128)S(1)}, u32[]{:S(2)}, u32[]{:S(2)}) collective-permute-start(f32[4,4,2,4,264]{4,3,2,1,0:T(4,128)S(1)} %get-tuple-element.13), channel_id=1, source_target_pairs={{2,0},{4,2},{6,4},{8,6},{10,8},{12,10},{14,12},{16,14},{18,16},{20... | collective-permute-start | bytes 405512 | tf_op jit(solution)/shard_map/ppermute | solution.py:23
  57.3 14.9 %collective-permute-start.8 = (f32[4,4,2,32,4]{4,3,2,1,0:T(8,128)S(1)}, f32[4,4,2,32,4]{4,3,2,1,0:T(8,128)S(1)}, u32[]{:S(2)}, u32[]{:S(2)}) collective-permute-start(f32[4,4,2,32,4]{4,3,2,1,0:T(8,128)S(1)} %get-tuple-element.30), channel_id=1, source_target_pairs={{0,32},{32,64},{64,96},{96,128},{128,160},{160,192},{192,224},{224... | collective-permute-start | bytes 49160 | tf_op jit(solution)/shard_map/ppermute | solution.py:22
  59.5 24.0 %collective-permute-start.9 = (f32[4,4,2,32,4]{4,3,2,1,0:T(8,128)S(1)}, f32[4,4,2,32,4]{4,3,2,1,0:T(8,128)S(1)}, u32[]{:S(2)}, u32[]{:S(2)}) collective-permute-start(f32[4,4,2,32,4]{4,3,2,1,0:T(8,128)S(1)} %get-tuple-element.31), channel_id=1, source_target_pairs={{32,0},{64,32},{96,64},{128,96},{160,128},{192,160},{224,192},{0,2... | collective-permute-start | bytes 49160 | tf_op jit(solution)/shard_map/ppermute | solution.py:23
  83.9 9.5 %collective-permute-start.10 = (f32[4,4,2,4,264]{4,3,2,1,0:T(4,128)S(1)}, f32[4,4,2,4,264]{4,3,2,1,0:T(4,128)S(1)}, u32[]{:S(2)}, u32[]{:S(2)}) collective-permute-start(f32[4,4,2,4,264]{4,3,2,1,0:T(4,128)S(1)} %get-tuple-element.10), channel_id=1, source_target_pairs={{0,2},{2,4},{4,6},{6,8},{8,10},{10,12},{12,14},{14,16},{16,18},{18... | collective-permute-start | bytes 405512 | tf_op jit(solution)/shard_map/ppermute | solution.py:22
  84.0 10.2 %collective-permute-start.11 = (f32[4,4,2,4,264]{4,3,2,1,0:T(4,128)S(1)}, f32[4,4,2,4,264]{4,3,2,1,0:T(4,128)S(1)}, u32[]{:S(2)}, u32[]{:S(2)}) collective-permute-start(f32[4,4,2,4,264]{4,3,2,1,0:T(4,128)S(1)} %get-tuple-element.11), channel_id=1, source_target_pairs={{2,0},{4,2},{6,4},{8,6},{10,8},{12,10},{14,12},{16,14},{18,16},{20... | collective-permute-start | bytes 405512 | tf_op jit(solution)/shard_map/ppermute | solution.py:23
  105.1 11.1 %copy-start.1 = (f32[4,4,2,32,256]{4,3,2,1,0:T(8,128)}, f32[4,4,2,32,256]{4,3,2,1,0:T(8,128)S(1)}, u32[]{:S(2)}) copy-start(f32[4,4,2,32,256]{4,3,2,1,0:T(8,128)S(1)} %fusion.24) | copy-start | bytes 3145732
  141.9 5.2 %all-to-all-start = ((f32[2,4,16384]{2,1,0:T(4,128)}), f32[2,4,16384]{2,1,0:T(4,128)S(1)}, u32[]{:S(2)}, u32[]{:S(2)}) async-start(f32[2,4,16384]{2,1,0:T(4,128)} %broadcast_in_dim.23), calls=%async_computation | async-start | bytes 1048576 | tf_op jit(solution)/shard_map/all_to_all | solution.py:30
where the time goes:
time: 190 us; the launch traced here: 189 us
  waiting for transfers between devices  51 us (27%)
  blocking collectives  40.3 us (21%)
  local copies, waits for them, and re-layouts  39.4 us (21%)
  starting transfers between devices  30.8 us (16%)
  other arithmetic  25 us (13%)
    psum x4, blocking collectives, one_axis_at_a_time(): shard = lax.psum(shard, axis)  40.3 us
    ppermute x6, waiting for transfers between devices, padded_2(): before = lax.ppermute(last, axis, up)  32.4 us
    gather x2, local copies, waits for them, and re-layouts, local(): samples = jnp.take(flat, site_cell[0, 0], axis=2)  24.5 us
    ppermute x6, starting transfers between devices, padded_2(): after = lax.ppermute(leading, axis, down)  19.3 us
    ppermute x6, waiting for transfers between devices, padded_2(): after = lax.ppermute(leading, axis, down)  17 us
    reshape x2, local copies, waits for them, and re-layouts, local(): flat = current.reshape(rep_local, CONST * 2, rows_lat * cols_lon)  11.1 us
    mul x5, other arithmetic, local(): window(wet_ext, width - 1)  8.83 us
    ppermute x6, starting transfers between devices, padded_2(): before = lax.ppermute(last, axis, up)  7.99 us
  transfers between devices with their start and end apart: 13, of which 9 were waited for; matrix products, arithmetic and copies ran while one was open for 1% of the time, Pallas kernels for 0%

commit v1 on v0

--- a/solution.py
+++ b/solution.py
@@ -43,7 +43,7 @@
 
 def one_axis_at_a_time(shard, axes):
     for axis in axes:
-        shard = lax.psum(shard, axis)
+        shard = jnp.sum(lax.all_gather(shard, axis), axis=0)
     return shard
 
 

time: 190 us -> 197 us (1.037)
  blocking collectives: 40.3 us -> 47.3 us
    all_gather x0 -> x4, blocking collectives: none -> 47.3 us  [one_axis_at_a_time(): shard = jnp.sum(lax.all_gather(shard, axis), axis=0)]
    psum x4 -> x0, blocking collectives: 40.3 us -> none  [one_axis_at_a_time(): shard = lax.psum(shard, axis)]
where the time goes in v1:
time: 197 us
  waiting for transfers between devices  51 us (26%)
  blocking collectives  47.3 us (24%)
  local copies, waits for them, and re-layouts  39.4 us (20%)
  starting transfers between devices  30.8 us (16%)
  other arithmetic  25.1 us (13%)
    all_gather x4, blocking collectives, one_axis_at_a_time(): shard = jnp.sum(lax.all_gather(shard, axis), axis=0)  47.3 us
    ppermute x6, waiting for transfers between devices, padded_2(): before = lax.ppermute(last, axis, up)  32.4 us
    gather x2, local copies, waits for them, and re-layouts, local(): samples = jnp.take(flat, site_cell[0, 0], axis=2)  24.5 us
    ppermute x6, starting transfers between devices, padded_2(): after = lax.ppermute(leading, axis, down)  19.3 us
    ppermute x6, waiting for transfers between devices, padded_2(): after = lax.ppermute(leading, axis, down)  17 us
    reshape x2, local copies, waits for them, and re-layouts, local(): flat = current.reshape(rep_local, CONST * 2, rows_lat * cols_lon)  11.1 us
    mul x5, other arithmetic, local(): window(wet_ext, width - 1)  8.83 us
    ppermute x6, starting transfers between devices, padded_2(): before = lax.ppermute(last, axis, up)  7.99 us
  transfers between devices with their start and end apart: 13, of which 9 were waited for; matrix products, arithmetic and copies ran while one was open for 1% of the time, Pallas kernels for 0%

profile of v1, /device:TPU:2, one launch (start us, length us, event | category | flops | bytes accessed | tf_op | source)
XLA Modules:
  0.0 196.5 jit_solution(9666463336009877773)
XLA Ops:
  0.7 0.8 convert_bitcast_fusion
  1.5 0.8 fusion.30
  2.3 1.6 collective-permute-start
  3.9 0.8 collective-permute-start.1
  4.7 1.4 fusion.35
  6.1 2.2 %collective-permute-start.4 = (f32[4,4,2,32,4]{4,3,2,1,0:T(8,128)S(1)}, f32[4,4,2,32,4]{4,3,2,1,0:T(8,128)S(1)}, u32[]{:S(2)}, u32[]{:S(2)}) collective-permute-start(f32[4,4,2,32,4]{4,3,2,1,0:T(8,128)S(1)} %get-tuple-element.32), channel_id=1, source_target_pairs={{0,32},{32,64},{64,96},{96,128},{128,160},{160,192},{192,224},{224... | collective-permute-start | bytes 49160 | tf_op jit(solution)/shard_map/ppermute | solution.py:22
  8.3 2.0 %collective-permute-start.5 = (f32[4,4,2,32,4]{4,3,2,1,0:T(8,128)S(1)}, f32[4,4,2,32,4]{4,3,2,1,0:T(8,128)S(1)}, u32[]{:S(2)}, u32[]{:S(2)}) collective-permute-start(f32[4,4,2,32,4]{4,3,2,1,0:T(8,128)S(1)} %get-tuple-element.33), channel_id=1, source_target_pairs={{32,0},{64,32},{96,64},{128,96},{160,128},{192,160},{224,192},{0,2... | collective-permute-start | bytes 49160 | tf_op jit(solution)/shard_map/ppermute | solution.py:23
  11.1 0.1 pad_maximum_fusion.10
  11.2 0.8 collective-permute-start.2
  12.0 5.4 %collective-permute-start.3 = (f32[2,4,264]{2,1,0:T(4,128)S(1)}, f32[2,4,264]{2,1,0:T(4,128)S(1)}, u32[]{:S(2)}, u32[]{:S(2)}) collective-permute-start(f32[2,4,264]{2,1,0:T(4,128)S(1)} %get-tuple-element.35), channel_id=1, source_target_pairs={{2,0},{4,2},{6,4},{8,6},{10,8},{12,10},{14,12},{16,14},{18,16},{20... | collective-permute-start | bytes 25352 | tf_op jit(solution)/shard_map/ppermute | solution.py:23
  17.4 13.3 %collective-permute-done.2 = f32[2,4,264]{2,1,0:T(4,128)S(1)} collective-permute-done((f32[2,4,264]{2,1,0:T(4,128)S(1)}, f32[2,4,264]{2,1,0:T(4,128)S(1)}, u32[]{:S(2)}, u32[]{:S(2)}) %collective-permute-start.2) | collective-permute-done | bytes 8480 | tf_op jit(solution)/shard_map/ppermute | solution.py:22
  30.7 2.9 %collective-permute-done.3 = f32[2,4,264]{2,1,0:T(4,128)S(1)} collective-permute-done((f32[2,4,264]{2,1,0:T(4,128)S(1)}, f32[2,4,264]{2,1,0:T(4,128)S(1)}, u32[]{:S(2)}, u32[]{:S(2)}) %collective-permute-start.3) | collective-permute-done | bytes 8480 | tf_op jit(solution)/shard_map/ppermute | solution.py:23
  33.6 0.1 maximum_multiply_fusion.10
  33.7 0.3 pad_maximum_fusion.5
  34.1 1.2 collective-permute-start.6
  35.3 5.6 %collective-permute-start.7 = (f32[4,4,2,4,264]{4,3,2,1,0:T(4,128)S(1)}, f32[4,4,2,4,264]{4,3,2,1,0:T(4,128)S(1)}, u32[]{:S(2)}, u32[]{:S(2)}) collective-permute-start(f32[4,4,2,4,264]{4,3,2,1,0:T(4,128)S(1)} %get-tuple-element.13), channel_id=1, source_target_pairs={{2,0},{4,2},{6,4},{8,6},{10,8},{12,10},{14,12},{16,14},{18,16},{20... | collective-permute-start | bytes 405512 | tf_op jit(solution)/shard_map/ppermute | solution.py:23
  40.8 0.1 slice.362
  41.0 0.1 slice.351
  41.4 2.8 %collective-permute-done.6 = f32[4,4,2,4,264]{4,3,2,1,0:T(4,128)S(1)} collective-permute-done((f32[4,4,2,4,264]{4,3,2,1,0:T(4,128)S(1)}, f32[4,4,2,4,264]{4,3,2,1,0:T(4,128)S(1)}, u32[]{:S(2)}, u32[]{:S(2)}) %collective-permute-start.6) | collective-permute-done | bytes 135200 | tf_op jit(solution)/shard_map/ppermute | solution.py:22
  44.2 2.0 %collective-permute-done.7 = f32[4,4,2,4,264]{4,3,2,1,0:T(4,128)S(1)} collective-permute-done((f32[4,4,2,4,264]{4,3,2,1,0:T(4,128)S(1)}, f32[4,4,2,4,264]{4,3,2,1,0:T(4,128)S(1)}, u32[]{:S(2)}, u32[]{:S(2)}) %collective-permute-start.7) | collective-permute-done | bytes 135200 | tf_op jit(solution)/shard_map/ppermute | solution.py:23
  46.2 1.0 broadcast_multiply_fusion.3
  47.2 0.6 multiply_subtract_fusion.5
  47.8 2.1 %broadcast_multiply_fusion.2 = (f32[4,4,2,38,262]{4,3,2,1,0:T(8,128)S(1)}, f32[4,4,2,38,262]{4,3,2,1,0:T(8,128)S(1)}) fusion(f32[38,262]{1,0:T(8,128)S(1)} %slice.362, f32[4,4,2,40,264]{4,3,2,1,0:T(8,128)S(1)} %get-tuple-element.8, f32[4,4,1,38,262]{4,3,2,1,0:T(8,128)S(1)} %get-tuple-element.29, f32[4,4,1,38,262]{4,3,2,1,0:T(8,128)S(1)} %get-tuple-element.28, ...), kind=kLoop, calls=%fused_computation.82 | loop fusion | flops 3185920 | bytes 10274592 | tf_op jit(solution)/shard_map/mul | solution.py:96
  50.0 0.6 multiply_subtract_fusion.4
  50.6 2.1 %broadcast_multiply_fusion.1 = (f32[4,4,2,36,260]{4,3,2,1,0:T(8,128)S(1)}, f32[4,4,2,36,260]{4,3,2,1,0:T(8,128)S(1)}) fusion(f32[36,260]{1,0:T(8,128)S(1)} %slice.370, f32[4,4,2,38,262]{4,3,2,1,0:T(8,128)S(1)} %get-tuple-element.6, f32[4,4,1,36,260]{4,3,2,1,0:T(8,128)S(1)} %get-tuple-element.27, f32[4,4,1,36,260]{4,3,2,1,0:T(8,128)S(1)} %get-tuple-element.26, ...), kind=kLoop, calls=%fused_computation.79 | loop fusion | flops 2995200 | bytes 9659520 | tf_op jit(solution)/shard_map/mul | solution.py:96
  52.7 0.6 multiply_subtract_fusion.3
  53.4 2.1 %broadcast_multiply_fusion = (f32[4,4,2,34,258]{4,3,2,1,0:T(8,128)S(1)}, f32[4,4,2,34,258]{4,3,2,1,0:T(8,128)S(1)}) fusion(f32[34,258]{1,0:T(8,128)S(1)} %slice.378, f32[4,4,2,36,260]{4,3,2,1,0:T(8,128)S(1)} %get-tuple-element.4, f32[4,4,1,34,258]{4,3,2,1,0:T(8,128)S(1)} %get-tuple-element.25, f32[4,4,1,34,258]{4,3,2,1,0:T(8,128)S(1)} %get-tuple-element.24, ...), kind=kLoop, calls=%fused_computation.78 | loop fusion | flops 2807040 | bytes 9052704 | tf_op jit(solution)/shard_map/mul | solution.py:96
  55.5 0.4 multiply_subtract_fusion.7
  55.9 1.2 fusion.27
  57.1 0.2 fusion.34
  57.3 2.1 %collective-permute-start.8 = (f32[4,4,2,32,4]{4,3,2,1,0:T(8,128)S(1)}, f32[4,4,2,32,4]{4,3,2,1,0:T(8,128)S(1)}, u32[]{:S(2)}, u32[]{:S(2)}) collective-permute-start(f32[4,4,2,32,4]{4,3,2,1,0:T(8,128)S(1)} %get-tuple-element.30), channel_id=1, source_target_pairs={{0,32},{32,64},{64,96},{96,128},{128,160},{160,192},{192,224},{224... | collective-permute-start | bytes 49160 | tf_op jit(solution)/shard_map/ppermute | solution.py:22
  59.5 12.7 %collective-permute-done.8 = f32[4,4,2,32,4]{4,3,2,1,0:T(8,128)S(1)} collective-permute-done((f32[4,4,2,32,4]{4,3,2,1,0:T(8,128)S(1)}, f32[4,4,2,32,4]{4,3,2,1,0:T(8,128)S(1)}, u32[]{:S(2)}, u32[]{:S(2)}) %collective-permute-start.8) | collective-permute-done | bytes 16416 | tf_op jit(solution)/shard_map/ppermute | solution.py:22
  72.2 11.3 %collective-permute-done.9 = f32[4,4,2,32,4]{4,3,2,1,0:T(8,128)S(1)} collective-permute-done((f32[4,4,2,32,4]{4,3,2,1,0:T(8,128)S(1)}, f32[4,4,2,32,4]{4,3,2,1,0:T(8,128)S(1)}, u32[]{:S(2)}, u32[]{:S(2)}) %collective-permute-start.9) | collective-permute-done | bytes 16416 | tf_op jit(solution)/shard_map/ppermute | solution.py:23
  83.5 0.3 pad_maximum_fusion.2
  83.9 0.1 collective-permute-start.10
  84.0 5.6 %collective-permute-start.11 = (f32[4,4,2,4,264]{4,3,2,1,0:T(4,128)S(1)}, f32[4,4,2,4,264]{4,3,2,1,0:T(4,128)S(1)}, u32[]{:S(2)}, u32[]{:S(2)}) collective-permute-start(f32[4,4,2,4,264]{4,3,2,1,0:T(4,128)S(1)} %get-tuple-element.11), channel_id=1, source_target_pairs={{2,0},{4,2},{6,4},{8,6},{10,8},{12,10},{14,12},{16,14},{18,16},{20... | collective-permute-start | bytes 405512 | tf_op jit(solution)/shard_map/ppermute | solution.py:23
  89.7 3.7 %collective-permute-done.10 = f32[4,4,2,4,264]{4,3,2,1,0:T(4,128)S(1)} collective-permute-done((f32[4,4,2,4,264]{4,3,2,1,0:T(4,128)S(1)}, f32[4,4,2,4,264]{4,3,2,1,0:T(4,128)S(1)}, u32[]{:S(2)}, u32[]{:S(2)}) %collective-permute-start.10) | collective-permute-done | bytes 135200 | tf_op jit(solution)/shard_map/ppermute | solution.py:22
  93.3 0.8 collective-permute-done.11
  94.2 0.9 maximum_multiply_fusion.4
  95.0 0.6 multiply_subtract_fusion.2
  95.7 2.2 %fusion.11 = f32[4,4,2,38,262]{4,3,2,1,0:T(8,128)S(1)} fusion(f32[4,4,2,40,264]{4,3,2,1,0:T(8,128)S(1)} %maximum_multiply_fusion.4, f32[4,4,1,38,262]{4,3,2,1,0:T(8,128)S(1)} %get-tuple-element.21, f32[4,4,1,38,262]{4,3,2,1,0:T(8,128)S(1)} %get-tuple-element.20, f32[38,262]{1,0:T(8,128)S(1)} %slice.362, f32[38,262]{1,0:T(8,128)S(1)} %slice.351), kind=kLoop, calls=%fused_computation.21 | loop fusion | flops 3185920 | bytes 9000224 | tf_op jit(solution)/shard_map/mul | solution.py:105
  97.8 0.6 multiply_subtract_fusion.1
  98.5 2.2 %fusion.7 = f32[4,4,2,36,260]{4,3,2,1,0:T(8,128)S(1)} fusion(f32[4,4,2,38,262]{4,3,2,1,0:T(8,128)S(1)} %fusion.11, f32[4,4,1,36,260]{4,3,2,1,0:T(8,128)S(1)} %get-tuple-element.19, f32[4,4,1,36,260]{4,3,2,1,0:T(8,128)S(1)} %get-tuple-element.18, f32[36,260]{1,0:T(8,128)S(1)} %slice.370, f32[36,260]{1,0:T(8,128)S(1)} %slice.350), kind=kLoop, calls=%fused_computation.13 | loop fusion | flops 2995200 | bytes 8461440 | tf_op jit(solution)/shard_map/mul | solution.py:105
  100.7 0.6 multiply_subtract_fusion
  101.3 2.2 %fusion.3 = f32[4,4,2,34,258]{4,3,2,1,0:T(8,128)S(1)} fusion(f32[4,4,2,36,260]{4,3,2,1,0:T(8,128)S(1)} %fusion.7, f32[4,4,1,34,258]{4,3,2,1,0:T(8,128)S(1)} %get-tuple-element.17, f32[4,4,1,34,258]{4,3,2,1,0:T(8,128)S(1)} %get-tuple-element.16, f32[34,258]{1,0:T(8,128)S(1)} %slice.378, f32[34,258]{1,0:T(8,128)S(1)} %slice.349), kind=kLoop, calls=%fused_computation.5 | loop fusion | flops 2807040 | bytes 7929888 | tf_op jit(solution)/shard_map/mul | solution.py:105
  103.5 0.4 multiply_subtract_fusion.6
  103.9 1.2 fusion.24
  105.1 0.2 reshape.141
  105.3 10.9 %copy.16 = f32[4,8,8192]{1,0,2:T(4,128)} copy(f32[4,8,8192]{2,1,0:T(8,128)S(1)} %reshape.141) | data formatting | bytes 2097152 | tf_op jit(solution)/shard_map/reshape | solution.py:111
  116.2 21.1 %gather_fusion = f32[2048,4,8]{2,1,0:T(4,128)} fusion(f32[4,8,8192]{1,0,2:T(4,128)} %copy.16, s32[2048]{0:T(1024)S(1)} %broadcast_clamp_fusion), kind=kCustom, calls=%fused_computation | custom fusion | bytes 532480 | tf_op jit(solution)/shard_map/jit(_take)/gather | solution.py:112
  137.3 3.4 %copy.17 = f32[2048,4,8]{0,2,1:T(8,128)S(1)} copy(f32[2048,4,8]{2,1,0:T(4,128)} %gather_fusion) | data formatting | bytes 524288 | tf_op jit(solution)/shard_map/jit(_take)/gather | solution.py:112
  140.7 0.2 copy.20
  140.9 0.1 broadcast_select_fusion
  141.0 0.9 broadcast_in_dim.23
  141.9 3.5 %all-to-all-start = ((f32[2,4,16384]{2,1,0:T(4,128)}), f32[2,4,16384]{2,1,0:T(4,128)S(1)}, u32[]{:S(2)}, u32[]{:S(2)}) async-start(f32[2,4,16384]{2,1,0:T(4,128)} %broadcast_in_dim.23), calls=%async_computation | async-start | bytes 1048576 | tf_op jit(solution)/shard_map/all_to_all | solution.py:30
  145.4 0.2 copy.18
  145.6 1.5 all-to-all-done
  147.1 0.2 reshape.142
  147.3 1.3 convolution_bitcast_fusion
  148.6 10.4 %all-gather.4 = f32[4,4,8]{2,1,0:T(4,128)S(1)} all-gather(f32[1,4,8]{2,1,0:T(4,128)S(1)} %convolution_bitcast_fusion), channel_id=2, replica_groups=mesh['lon_0'=4,'lon_1'=2,'lat_0'=8,'lat_1'=2,'rep'=2] {'lon_0'}, dimensions={0}, use_global_device_ids=true | all-gather | bytes 640 | tf_op jit(solution)/shard_map/all_gather | solution.py:46
  159.0 4.4 %all-gather.5 = f32[2,4,8]{2,1,0:T(4,128)S(1)} all-gather(f32[1,4,8]{2,1,0:T(4,128)S(1)} %bitcast.49), channel_id=3, replica_groups=mesh['lon_0'=4,'lon_1'=2,'lat_0'=8,'lat_1'=2,'rep'=2] {'lon_1'}, dimensions={0}, use_global_device_ids=true | all-gather | bytes 384 | tf_op jit(solution)/shard_map/all_gather | solution.py:46
  163.4 26.6 %all-gather.6 = f32[8,4,8]{2,1,0:T(4,128)S(1)} all-gather(f32[1,4,8]{2,1,0:T(4,128)S(1)} %bitcast.48), channel_id=4, replica_groups=mesh['lon_0'=4,'lon_1'=2,'lat_0'=8,'lat_1'=2,'rep'=2] {'lat_0'}, dimensions={0}, use_global_device_ids=true | all-gather | bytes 1152 | tf_op jit(solution)/shard_map/all_gather | solution.py:46
  190.1 5.9 %all-gather.7 = f32[2,4,8]{2,1,0:T(4,128)S(1)} all-gather(f32[1,4,8]{2,1,0:T(4,128)S(1)} %bitcast.47), channel_id=5, replica_groups=mesh['lon_0'=4,'lon_1'=2,'lat_0'=8,'lat_1'=2,'rep'=2] {'lat_1'}, dimensions={0}, use_global_device_ids=true | all-gather | bytes 384 | tf_op jit(solution)/shard_map/all_gather | solution.py:46
  195.9 0.6 broadcast_multiply_fusion.4
  (38 shorter events, 0.7 us)
Async XLA Ops:
  0.6 10.5 %copy-start.2 = (f32[32,256]{1,0:T(8,128)S(1)}, f32[32,256]{1,0:T(8,128)}, u32[]{:S(2)}) copy-start(f32[32,256]{1,0:T(8,128)} %param.8) | copy-start | bytes 98308
  0.6 33.1 %copy-start = (f32[4,4,2,32,256]{4,3,2,1,0:T(8,128)S(1)}, f32[4,4,2,32,256]{4,3,2,1,0:T(8,128)}, u32[]{:S(2)}) copy-start(f32[4,4,2,32,256]{4,3,2,1,0:T(8,128)} %param.7) | copy-start | bytes 3145732
  0.7 9.7 %copy-start.3 = (s32[1,1,2048]{2,1,0:T(1,128)S(1)}, s32[1,1,2048]{2,1,0:T(1,128)}, u32[]{:S(2)}) copy-start(s32[1,1,2048]{2,1,0:T(1,128)} %param.11) | copy-start | bytes 24580
  0.7 10.3 %copy-start.4 = (f32[1,1,2048]{2,1,0:T(1,128)S(1)}, f32[1,1,2048]{2,1,0:T(1,128)}, u32[]{:S(2)}) copy-start(f32[1,1,2048]{2,1,0:T(1,128)} %param.13) | copy-start | bytes 24580
  0.7 10.3 %copy-start.5 = (f32[4]{0:T(128)S(1)}, f32[4]{0:T(128)}, u32[]{:S(2)}) copy-start(f32[4]{0:T(128)} %param.10) | copy-start | bytes 52
  2.3 8.7 %collective-permute-start = (f32[2,32,4]{2,1,0:T(8,128)S(1)}, f32[2,32,4]{2,1,0:T(8,128)S(1)}, u32[]{:S(2)}, u32[]{:S(2)}) collective-permute-start(f32[2,32,4]{2,1,0:T(8,128)S(1)} %get-tuple-element.38), channel_id=1, source_target_pairs={{0,32},{32,64},{64,96},{96,128},{128,160},{160,192},{192,224},{224... | collective-permute-start | bytes 3080 | tf_op jit(solution)/shard_map/ppermute | solution.py:22
  3.9 7.2 %collective-permute-start.1 = (f32[2,32,4]{2,1,0:T(8,128)S(1)}, f32[2,32,4]{2,1,0:T(8,128)S(1)}, u32[]{:S(2)}, u32[]{:S(2)}) collective-permute-start(f32[2,32,4]{2,1,0:T(8,128)S(1)} %get-tuple-element.39), channel_id=1, source_target_pairs={{32,0},{64,32},{96,64},{128,96},{160,128},{192,160},{224,192},{0,2... | collective-permute-start | bytes 3080 | tf_op jit(solution)/shard_map/ppermute | solution.py:23
  6.1 27.6 %collective-permute-start.4 = (f32[4,4,2,32,4]{4,3,2,1,0:T(8,128)S(1)}, f32[4,4,2,32,4]{4,3,2,1,0:T(8,128)S(1)}, u32[]{:S(2)}, u32[]{:S(2)}) collective-permute-start(f32[4,4,2,32,4]{4,3,2,1,0:T(8,128)S(1)} %get-tuple-element.32), channel_id=1, source_target_pairs={{0,32},{32,64},{64,96},{96,128},{128,160},{160,192},{192,224},{224... | collective-permute-start | bytes 49160 | tf_op jit(solution)/shard_map/ppermute | solution.py:22
  8.3 25.4 %collective-permute-start.5 = (f32[4,4,2,32,4]{4,3,2,1,0:T(8,128)S(1)}, f32[4,4,2,32,4]{4,3,2,1,0:T(8,128)S(1)}, u32[]{:S(2)}, u32[]{:S(2)}) collective-permute-start(f32[4,4,2,32,4]{4,3,2,1,0:T(8,128)S(1)} %get-tuple-element.33), channel_id=1, source_target_pairs={{32,0},{64,32},{96,64},{128,96},{160,128},{192,160},{224,192},{0,2... | collective-permute-start | bytes 49160 | tf_op jit(solution)/shard_map/ppermute | solution.py:23
  11.2 19.5 %collective-permute-start.2 = (f32[2,4,264]{2,1,0:T(4,128)S(1)}, f32[2,4,264]{2,1,0:T(4,128)S(1)}, u32[]{:S(2)}, u32[]{:S(2)}) collective-permute-start(f32[2,4,264]{2,1,0:T(4,128)S(1)} %get-tuple-element.34), channel_id=1, source_target_pairs={{0,2},{2,4},{4,6},{6,8},{8,10},{10,12},{12,14},{14,16},{16,18},{18... | collective-permute-start | bytes 25352 | tf_op jit(solution)/shard_map/ppermute | solution.py:22
  12.0 21.6 %collective-permute-start.3 = (f32[2,4,264]{2,1,0:T(4,128)S(1)}, f32[2,4,264]{2,1,0:T(4,128)S(1)}, u32[]{:S(2)}, u32[]{:S(2)}) collective-permute-start(f32[2,4,264]{2,1,0:T(4,128)S(1)} %get-tuple-element.35), channel_id=1, source_target_pairs={{2,0},{4,2},{6,4},{8,6},{10,8},{12,10},{14,12},{16,14},{18,16},{20... | collective-permute-start | bytes 25352 | tf_op jit(solution)/shard_map/ppermute | solution.py:23
  34.1 10.1 %collective-permute-start.6 = (f32[4,4,2,4,264]{4,3,2,1,0:T(4,128)S(1)}, f32[4,4,2,4,264]{4,3,2,1,0:T(4,128)S(1)}, u32[]{:S(2)}, u32[]{:S(2)}) collective-permute-start(f32[4,4,2,4,264]{4,3,2,1,0:T(4,128)S(1)} %get-tuple-element.12), channel_id=1, source_target_pairs={{0,2},{2,4},{4,6},{6,8},{8,10},{10,12},{12,14},{14,16},{16,18},{18... | collective-permute-start | bytes 405512 | tf_op jit(solution)/shard_map/ppermute | solution.py:22
  35.3 10.9 %collective-permute-start.7 = (f32[4,4,2,4,264]{4,3,2,1,0:T(4,128)S(1)}, f32[4,4,2,4,264]{4,3,2,1,0:T(4,128)S(1)}, u32[]{:S(2)}, u32[]{:S(2)}) collective-permute-start(f32[4,4,2,4,264]{4,3,2,1,0:T(4,128)S(1)} %get-tuple-element.13), channel_id=1, source_target_pairs={{2,0},{4,2},{6,4},{8,6},{10,8},{12,10},{14,12},{16,14},{18,16},{20... | collective-permute-start | bytes 405512 | tf_op jit(solution)/shard_map/ppermute | solution.py:23
  57.3 14.9 %collective-permute-start.8 = (f32[4,4,2,32,4]{4,3,2,1,0:T(8,128)S(1)}, f32[4,4,2,32,4]{4,3,2,1,0:T(8,128)S(1)}, u32[]{:S(2)}, u32[]{:S(2)}) collective-permute-start(f32[4,4,2,32,4]{4,3,2,1,0:T(8,128)S(1)} %get-tuple-element.30), channel_id=1, source_target_pairs={{0,32},{32,64},{64,96},{96,128},{128,160},{160,192},{192,224},{224... | collective-permute-start | bytes 49160 | tf_op jit(solution)/shard_map/ppermute | solution.py:22
  59.5 24.0 %collective-permute-start.9 = (f32[4,4,2,32,4]{4,3,2,1,0:T(8,128)S(1)}, f32[4,4,2,32,4]{4,3,2,1,0:T(8,128)S(1)}, u32[]{:S(2)}, u32[]{:S(2)}) collective-permute-start(f32[4,4,2,32,4]{4,3,2,1,0:T(8,128)S(1)} %get-tuple-element.31), channel_id=1, source_target_pairs={{32,0},{64,32},{96,64},{128,96},{160,128},{192,160},{224,192},{0,2... | collective-permute-start | bytes 49160 | tf_op jit(solution)/shard_map/ppermute | solution.py:23
  83.9 9.5 %collective-permute-start.10 = (f32[4,4,2,4,264]{4,3,2,1,0:T(4,128)S(1)}, f32[4,4,2,4,264]{4,3,2,1,0:T(4,128)S(1)}, u32[]{:S(2)}, u32[]{:S(2)}) collective-permute-start(f32[4,4,2,4,264]{4,3,2,1,0:T(4,128)S(1)} %get-tuple-element.10), channel_id=1, source_target_pairs={{0,2},{2,4},{4,6},{6,8},{8,10},{10,12},{12,14},{14,16},{16,18},{18... | collective-permute-start | bytes 405512 | tf_op jit(solution)/shard_map/ppermute | solution.py:22
  84.0 10.2 %collective-permute-start.11 = (f32[4,4,2,4,264]{4,3,2,1,0:T(4,128)S(1)}, f32[4,4,2,4,264]{4,3,2,1,0:T(4,128)S(1)}, u32[]{:S(2)}, u32[]{:S(2)}) collective-permute-start(f32[4,4,2,4,264]{4,3,2,1,0:T(4,128)S(1)} %get-tuple-element.11), channel_id=1, source_target_pairs={{2,0},{4,2},{6,4},{8,6},{10,8},{12,10},{14,12},{16,14},{18,16},{20... | collective-permute-start | bytes 405512 | tf_op jit(solution)/shard_map/ppermute | solution.py:23
  105.1 11.1 %copy-start.1 = (f32[4,4,2,32,256]{4,3,2,1,0:T(8,128)}, f32[4,4,2,32,256]{4,3,2,1,0:T(8,128)S(1)}, u32[]{:S(2)}) copy-start(f32[4,4,2,32,256]{4,3,2,1,0:T(8,128)S(1)} %fusion.24) | copy-start | bytes 3145732
  141.9 5.2 %all-to-all-start = ((f32[2,4,16384]{2,1,0:T(4,128)}), f32[2,4,16384]{2,1,0:T(4,128)S(1)}, u32[]{:S(2)}, u32[]{:S(2)}) async-start(f32[2,4,16384]{2,1,0:T(4,128)} %broadcast_in_dim.23), calls=%async_computation | async-start | bytes 1048576 | tf_op jit(solution)/shard_map/all_to_all | solution.py:30
